TPU v7x, 32 devices: a whole 2x2x4 slice. The times are simulated.
32 devices in a mesh: groups: 2 (over y), block: 4 (over x, core), tensor: 4 (over z).
Axes of the slice: x: 2, y: 2, z: 4, core: 2. Of those that a mesh axis runs over, the one named last changes fastest.
Arguments:
- tokens: bfloat16 [4096, 5120], P(('groups', 'block', 'tensor')), parts along dimension 0, may hold values from -20 to 20
- mod_shift: float32 [5120], replicated, may hold values from -3 to 3
- mod_scale: float32 [5120], replicated, may hold values from -0.5 to 0.5
- w_qkv: bfloat16 [3, 5120, 1024], P(None, 'block', 'tensor'), may hold values from -1 to 1
- tile_list: int32 [8, 4, 5], P(('groups', 'block')), parts along dimension 0, may hold values from 0 to 7, as said below
- tile_count: int32 [8, 4], P(('groups', 'block')), parts along dimension 0, may hold values from 2 to 5, as said below
Outputs:
- attended: bfloat16 [4096, 1024], P(('groups', 'block'), 'tensor'), parts along dimension 0
There are 2 independent parts, one for each index of `groups`. A program takes and returns all parts, laid end to end along the dimension named above; an argument that names none is the same for every part. Nothing has to cross between parts.
Inputs may be any that keep to these rules, and one draw needn't show every extreme that they name: `tile_list`: within the first tile_count[c, t] slots the entries are distinct, the first is the query tile itself (2 + t), and none names a tile outside the slab; blocks at scene cuts name no tile of the block across the cut. Later slots hold indices in range and are not read. `tile_count`: the first query tile of every block reads 5 slots.
All inputs are finite; a program needn't handle non-finite values.
Results may differ from a plain program's by a relative error of at most 0.0087.
Values may be sent and summed in bfloat16 or wider, within the bound.
No kernel may reach another device: no remote copies, remote signals or barrier semaphores. Data moves between devices by JAX's collectives and lax.ppermute only.
A program may use at most 64 MiB of HBM per device.

v0:
```python
import jax
import jax.numpy as jnp
from jax import lax
from jax.sharding import PartitionSpec as P

HEAD_DIM = 128
TILE = 128
BT = 2
epsilon = 1e-06


def with_halo(x, sides, width):
    for axis, dim in sides:
        count, length = (lax.axis_size(axis), x.shape[dim])
        up = [(i, (i + 1) % count) for i in range(count - 1)]
        down = [(j, i) for i, j in up]
        last = lax.slice_in_dim(x, length - width, length, axis=dim)
        first = lax.slice_in_dim(x, 0, width, axis=dim)
        before = lax.ppermute(last, axis, up)
        after = lax.ppermute(first, axis, down)
        x = jnp.concatenate([before, x, after], axis=dim)
    return x


def attend(queries, key_rows, value_rows, chosen_list, chosen_count):
    head_count = queries.shape[1] // HEAD_DIM
    local_tiles = queries.shape[0] // TILE
    all_tiles = key_rows.shape[0] // TILE
    slot_count = chosen_list.shape[1]
    shaped_queries = queries.reshape(local_tiles, TILE, head_count, HEAD_DIM)
    key_tiles = key_rows.reshape(all_tiles, TILE, head_count, HEAD_DIM)[chosen_list]
    value_tiles = value_rows.reshape(all_tiles, TILE, head_count, HEAD_DIM)[chosen_list]
    scores = jnp.einsum(
        "pthd,pkshd->phtks", shaped_queries, key_tiles, preferred_element_type=jnp.float32
    )
    scores = scores * HEAD_DIM ** (-0.5)
    live_slot = jnp.arange(slot_count, dtype=jnp.int32)[None, :] < chosen_count[:, None]
    scores = jnp.where(live_slot[:, None, None, :, None], scores, jnp.float32(-1e30))
    highest = jnp.max(scores, axis=(3, 4), keepdims=True)
    exponent = jnp.exp(scores - highest)
    denominator = jnp.sum(exponent, axis=(3, 4), keepdims=True)
    attn_weights = (exponent / denominator).astype(jnp.bfloat16)
    mixed = jnp.einsum(
        "phtks,pkshd->pthd", attn_weights, value_tiles, preferred_element_type=jnp.float32
    )
    return mixed.astype(jnp.bfloat16).reshape(local_tiles * TILE, head_count * HEAD_DIM)


def shards(tokens, mod_shift, mod_scale, w_qkv, tile_list, tile_count):
    values_in = tokens.astype(jnp.float32)
    row_mean = jnp.mean(values_in, axis=1, keepdims=True)
    centred = values_in - row_mean
    row_var = jnp.mean(centred * centred, axis=1, keepdims=True)
    normed = (centred * lax.rsqrt(row_var + epsilon) * (1.0 + mod_scale) + mod_shift).astype(
        jnp.bfloat16
    )
    gathered = lax.all_gather(normed, "tensor", axis=0, tiled=True)
    projected = jnp.einsum(
        "td,ide->ite",
        gathered,
        lax.all_gather(w_qkv, "block", axis=1, tiled=True),
        preferred_element_type=jnp.float32,
    )
    projected = projected.astype(jnp.bfloat16)
    queries = projected[0]
    key_value = projected[1:3]
    extended = with_halo(key_value, (("block", 1),), BT * TILE)
    return attend(queries, extended[0], extended[1], tile_list[0], tile_count[0])


def solution(mesh):
    return jax.shard_map(
        shards,
        mesh=mesh,
        in_specs=(
            P(("groups", "block", "tensor"), None),
            P(),
            P(),
            P(None, "block", "tensor"),
            P(("groups", "block"), None, None),
            P(("groups", "block"), None),
        ),
        out_specs=P(("groups", "block"), "tensor"),
        check_vma=False,
    )
```

profile of v0, /device:TPU:1, one launch (start us, length us, event | category | flops | bytes accessed | tf_op | source)
XLA Modules:
  0.0 203.5 jit_solution(6897856617463823574)
XLA Ops:
  6.5 0.0 copy-start
  6.5 0.0 copy-start.2
  6.5 0.0 copy-start.1
  6.5 0.0 all-gather.3.cloned.1.call-start
  6.5 1.7 convert_reduce_fusion
  8.2 1.8 fusion.4
  10.1 0.0 copy-done.2
  10.1 0.0 copy-done
  10.1 0.0 copy-done.1
  10.1 0.0 copy-start.3
  10.1 1.7 fusion.7
  11.8 0.0 all-gather.3.cloned.1.call-update
  11.8 0.0 all-gather.5.cloned.1.call-start
  11.9 0.7 all-gather.5.cloned.1.call-update
  12.6 0.0 copy-done.3
  12.6 0.1 reshape.73
  12.7 0.0 copy-start.4
  12.7 99.4 %all-gather.3.cloned.1.call-done = bf16[512,5120]{1,0:T(8,128)(2,1)} async-done(((bf16[128,5120]{1,0:T(8,128)(2,1)}), bf16[512,5120]{1,0:T(8,128)(2,1)}) %all-gather.3.cloned.1.call-update) | async-done | bytes 5242896 | tf_op jit(solution)/shard_map/all_gather | solution.py:57
  112.1 55.6 %all-gather.5.cloned.1.call-done = bf16[3,5120,256]{2,1,0:T(8,128)(2,1)} async-done(((bf16[3,1280,256]{2,1,0:T(8,128)(2,1)}), bf16[3,5120,256]{2,1,0:T(8,128)(2,1)}) %all-gather.5.cloned.1.call-update) | async-done | bytes 7864336 | tf_op jit(solution)/shard_map/all_gather | solution.py:61
  167.7 9.0 %fusion.16 = bf16[3,512,256]{2,1,0:T(8,128)(2,1)S(1)} fusion(bf16[3,5120,256]{2,1,0:T(8,128)(2,1)} %all-gather.5.cloned.1.call-done, bf16[512,5120]{1,0:T(8,128)(2,1)} %all-gather.3.cloned.1.call-done), kind=kOutput, calls=%fused_computation.21 | convolution fusion | flops 4026925056 | bytes 13893632 | tf_op jit(solution)/shard_map/td,ide->ite/dot_general | solution.py:58
  176.7 2.1 %collective-permute-start = (bf16[2,256,256]{2,1,0:T(8,128)(2,1)S(1)}, bf16[2,256,256]{2,1,0:T(8,128)(2,1)S(1)}, u32[]{:S(2)}, u32[]{:S(2)}) collective-permute-start(bf16[2,256,256]{2,1,0:T(8,128)(2,1)S(1)} %get-tuple-element.7), channel_id=1, source_target_pairs={{0,4},{4,8},{8,12},{1,5},{5,9},{9,13},{2,6},{6,10},{10,14},{3,7},{... | collective-permute-start | bytes 786440 | tf_op jit(solution)/shard_map/ppermute | solution.py:19
  178.9 2.2 %collective-permute-start.1 = (bf16[2,256,256]{2,1,0:T(8,128)(2,1)S(1)}, bf16[2,256,256]{2,1,0:T(8,128)(2,1)S(1)}, u32[]{:S(2)}, u32[]{:S(2)}) collective-permute-start(bf16[2,256,256]{2,1,0:T(8,128)(2,1)S(1)} %get-tuple-element.8), channel_id=1, source_target_pairs={{4,0},{8,4},{12,8},{5,1},{9,5},{13,9},{6,2},{10,6},{14,10},{7,3},{... | collective-permute-start | bytes 786440 | tf_op jit(solution)/shard_map/ppermute | solution.py:20
  181.1 0.0 copy-done.4
  181.1 0.1 iota_compare_fusion
  181.3 0.1 reshape_squeeze.10
  181.3 0.8 collective-permute-done
  182.2 4.4 %collective-permute-done.1 = bf16[2,256,256]{2,1,0:T(8,128)(2,1)S(1)} collective-permute-done((bf16[2,256,256]{2,1,0:T(8,128)(2,1)S(1)}, bf16[2,256,256]{2,1,0:T(8,128)(2,1)S(1)}, u32[]{:S(2)}, u32[]{:S(2)}) %collective-permute-start.1) | collective-permute-done | bytes 262176 | tf_op jit(solution)/shard_map/ppermute | solution.py:20
  186.6 0.1 pad_maximum_fusion
  186.6 0.1 fusion.32
  186.7 0.1 reshape_squeeze.11
  186.9 0.1 copy.15
  187.0 0.8 gather_fusion.1
  187.8 0.1 copy.17
  187.9 0.5 fusion.28
  188.4 0.4 fusion.8
  188.8 0.6 fusion.9
  189.4 0.9 reshape_squeeze.9
  190.3 1.1 copy.14
  191.5 1.9 gather_fusion
  193.3 2.4 %fusion.25 = bf16[4,128,2,128]{1,3,2,0:T(8,128)(2,1)S(1)} fusion(f32[4,2,128,5,128]{2,4,3,1,0:T(8,128)S(1)} %bitcast.38, f32[4,2,128]{2,1,0:T(2,128)S(1)} %fusion.9, f32[4,2,128]{2,1,0:T(2,128)S(1)} %fusion.8, pred[4,5]{1,0:T(4,128)(4,1)S(1)} %iota_compare_fusion, bf16[4,5,128,2,128]{4,2,3,1,0:T(8,128)(2,1)} %bitcast.41), kind=kOutput, calls=%fused_computation.24 | convolution fusion | flops 171180032 | bytes 4202516 | tf_op jit(solution)/shard_map/phtks,pkshd->pthd/dot_general | solution.py:43
  195.8 0.2 copy.20
  195.9 0.7 copy.37
  (8 shorter events, 0.1 us)
Async XLA Ops:
  6.5 3.6 %copy-start = (bf16[128,5120]{1,0:T(8,128)(2,1)S(1)}, bf16[128,5120]{1,0:T(8,128)(2,1)}, u32[]{:S(2)}) copy-start(bf16[128,5120]{1,0:T(8,128)(2,1)} %param.6) | copy-start | bytes 3932164
  6.5 3.5 %copy-start.2 = (f32[5120]{0:T(1024)S(1)}, f32[5120]{0:T(1024)}, u32[]{:S(2)}) copy-start(f32[5120]{0:T(1024)} %param.8) | copy-start | bytes 61444
  6.5 3.6 %copy-start.1 = (f32[5120]{0:T(1024)S(1)}, f32[5120]{0:T(1024)}, u32[]{:S(2)}) copy-start(f32[5120]{0:T(1024)} %param.7) | copy-start | bytes 61444
  6.5 105.5 %all-gather.3.cloned.1.call-start = ((), (), s32[]{:S(2)}) async-start(), calls=%async_computation | async-start | bytes 6553600 | tf_op jit(solution)/shard_map/all_gather | solution.py:57
  10.1 2.4 %copy-start.3 = (s32[1,4,5]{2,1,0:T(4,128)S(1)}, s32[1,4,5]{2,1,0:T(4,128)}, u32[]{:S(2)}) copy-start(s32[1,4,5]{2,1,0:T(4,128)} %param.10) | copy-start | bytes 244
  11.8 155.9 %all-gather.5.cloned.1.call-start = ((), (), s32[]{:S(2)}) async-start(), calls=%async_computation.1 | async-start | bytes 9830400 | tf_op jit(solution)/shard_map/all_gather | solution.py:61
  12.7 168.5 %copy-start.4 = (s32[1,4]{1,0:T(1,128)S(1)}, s32[1,4]{1,0:T(1,128)}, u32[]{:S(2)}) copy-start(s32[1,4]{1,0:T(1,128)} %param.11) | copy-start | bytes 52
  176.7 5.4 %collective-permute-start = (bf16[2,256,256]{2,1,0:T(8,128)(2,1)S(1)}, bf16[2,256,256]{2,1,0:T(8,128)(2,1)S(1)}, u32[]{:S(2)}, u32[]{:S(2)}) collective-permute-start(bf16[2,256,256]{2,1,0:T(8,128)(2,1)S(1)} %get-tuple-element.7), channel_id=1, source_target_pairs={{0,4},{4,8},{8,12},{1,5},{5,9},{9,13},{2,6},{6,10},{10,14},{3,7},{... | collective-permute-start | bytes 786440 | tf_op jit(solution)/shard_map/ppermute | solution.py:19
  178.9 7.7 %collective-permute-start.1 = (bf16[2,256,256]{2,1,0:T(8,128)(2,1)S(1)}, bf16[2,256,256]{2,1,0:T(8,128)(2,1)S(1)}, u32[]{:S(2)}, u32[]{:S(2)}) collective-permute-start(bf16[2,256,256]{2,1,0:T(8,128)(2,1)S(1)} %get-tuple-element.8), channel_id=1, source_target_pairs={{4,0},{8,4},{12,8},{5,1},{9,5},{13,9},{6,2},{10,6},{14,10},{7,3},{... | collective-permute-start | bytes 786440 | tf_op jit(solution)/shard_map/ppermute | solution.py:20
Sparse Core Ops, SparseCore 0:
  11.9 100.1 all-gather.2
  113.6 54.0 all-gather.4
where the time goes:
time: 204 us
  waiting for transfers between devices  161 us (79%)
  between operations  13.6 us (7%)
  matrix products  11.9 us (6%)
  other arithmetic  6.35 us (3%)
  local copies, waits for them, and re-layouts  6.3 us (3%)
  starting transfers between devices  4.38 us (2%)
    all_gather x1, waiting for transfers between devices, shards(): gathered = lax.all_gather(normed, 'tensor', axis=0, tiled=True)  99.4 us
    all_gather x1, waiting for transfers between devices, shards(): lax.all_gather(w_qkv, 'block', axis=1, tiled=True)  55.6 us
    dot_general x1, matrix products, shards(): jnp.einsum('td,ide->ite', gathered, lax.all_gather(w_qkv, 'block', axis=1...  9.01 us
    ppermute x1, waiting for transfers between devices, with_halo(): after = lax.ppermute(first, axis, down)  4.4 us
  transfers between devices with their start and end apart: 4, of which 4 were waited for; matrix products, arithmetic and copies ran while one was open for 0% of the time, Pallas kernels for 0%

commit v1 on v0

--- a/solution.py
+++ b/solution.py
@@ -54,7 +54,25 @@
     normed = (centred * lax.rsqrt(row_var + epsilon) * (1.0 + mod_scale) + mod_shift).astype(
         jnp.bfloat16
     )
-    gathered = lax.all_gather(normed, "tensor", axis=0, tiled=True)
+    arr_next = jax.lax.axis_index("tensor")
+    found_now = jax.lax.axis_size("tensor")
+    v_next, next_value, low = (found_now, arr_next, normed.shape[0])
+    lanes = [(it, (it + 1) % v_next) for it in range(v_next)]
+    views = [(it, (it - 1) % v_next) for it in range(v_next)]
+    gathered = jnp.zeros((*normed.shape[:0], v_next * low, *normed.shape[1:]), normed.dtype)
+    oldest = answer = normed
+    part_next = v_next // 2
+    gathered = lax.dynamic_update_slice_in_dim(gathered, normed, next_value * low, axis=0)
+    for nth in tuple(range(1, part_next + 1)):
+        oldest = jax.lax.ppermute(oldest, axis_name="tensor", perm=lanes)
+        gathered = lax.dynamic_update_slice_in_dim(
+            gathered, oldest, (next_value - nth) % v_next * low, axis=0
+        )
+        if nth < v_next - part_next:
+            answer = jax.lax.ppermute(answer, axis_name="tensor", perm=views)
+            gathered = lax.dynamic_update_slice_in_dim(
+                gathered, answer, (next_value + nth) % v_next * low, axis=0
+            )
     projected = jnp.einsum(
         "td,ide->ite",
         gathered,

time: 204 us -> 142 us (0.70)
  waiting for transfers between devices: 161 us -> 85.6 us
  local copies, waits for them, and re-layouts: 6.3 us -> 16 us
  starting transfers between devices: 4.38 us -> 12 us
  other arithmetic: 6.35 us -> 2.6 us
    all_gather x1 -> x0, waiting for transfers between devices: 99.4 us -> none  [shards(): gathered = lax.all_gather(normed, 'tensor', axis=0, tiled=True)]
    ppermute x0 -> x3, waiting for transfers between devices: none -> 79.4 us  [the longest x2 52.9 us: shards(): oldest = jax.lax.ppermute(oldest, axis_name='tensor', perm=lanes)]
    all_gather x1, waiting for transfers between devices: 55.6 us -> 0.01 us  [shards(): lax.all_gather(w_qkv, 'block', axis=1, tiled=True)]
    dynamic_update_slice x0 -> x3, local copies, waits for them, and re-layouts: none -> 6.1 us  [the longest x2 3.66 us: shards(): lax.dynamic_update_slice_in_dim(gathered, oldest, (next_value - nth) % v_...]
    ppermute x0 -> x3, starting transfers between devices: none -> 4.14 us  [the longest x2 2.12 us: shards(): oldest = jax.lax.ppermute(oldest, axis_name='tensor', perm=lanes)]
    ppermute x1, starting transfers between devices: 2.12 us -> 5.93 us  [with_halo(): before = lax.ppermute(last, axis, up)]
    unnamed x11 -> x13, local copies, waits for them, and re-layouts: 0.76 us -> 3.73 us
  transfers between devices with their start and end apart: 4 -> 6, of which waited for: 4 -> 5; matrix products, arithmetic and copies ran while one was open for 0% -> 6% of each run, Pallas kernels for 0% -> 0%
where the time goes in v1:
time: 142 us
  waiting for transfers between devices  85.6 us (60%)
  local copies, waits for them, and re-layouts  16 us (11%)
  between operations  13.6 us (10%)
  starting transfers between devices  12 us (8%)
  matrix products  11.9 us (8%)
  other arithmetic  2.6 us (2%)
    ppermute x2, waiting for transfers between devices, shards(): oldest = jax.lax.ppermute(oldest, axis_name='tensor', perm=lanes)  52.9 us
    ppermute x1, waiting for transfers between devices, shards(): answer = jax.lax.ppermute(answer, axis_name='tensor', perm=views)  26.5 us
    dot_general x1, matrix products, shards(): jnp.einsum('td,ide->ite', gathered, lax.all_gather(w_qkv, 'block', axis=1...  9.02 us
    ppermute x1, starting transfers between devices, with_halo(): before = lax.ppermute(last, axis, up)  5.93 us
    ppermute x1, waiting for transfers between devices, with_halo(): after = lax.ppermute(first, axis, down)  4.4 us
    unnamed x13, local copies, waits for them, and re-layouts  3.73 us
    dynamic_update_slice x2, local copies, waits for them, and re-layouts, shards(): lax.dynamic_update_slice_in_dim(gathered, oldest, (next_value - nth) % v_...  3.66 us
  transfers between devices with their start and end apart: 6, of which 5 were waited for; matrix products, arithmetic and copies ran while one was open for 6% of the time, Pallas kernels for 0%

profile of v1, /device:TPU:1, one launch (start us, length us, event | category | flops | bytes accessed | tf_op | source)
XLA Modules:
  0.0 141.8 jit_solution(472594483574026436)
XLA Ops:
  6.5 0.0 copy-start
  6.5 0.0 copy-start.3
  6.5 0.0 all-gather.2.cloned.1.call-start
  6.5 0.7 all-gather.2.cloned.1.call-update
  7.3 0.6 copy-done
  7.9 0.3 convert_reduce_fusion
  8.1 0.5 fusion.4
  8.6 0.0 copy-done.3
  8.7 0.0 copy-start.2
  8.7 0.6 broadcast_in_dim.10
  9.3 0.1 copy-done.2
  9.4 0.0 copy-start.4
  9.4 0.6 constant_dynamic-update-slice_fusion.3
  10.0 0.0 copy-start.1
  10.1 2.3 %copy-done.1 = bf16[512,5120]{1,0:T(8,128)(2,1)} copy-done((bf16[512,5120]{1,0:T(8,128)(2,1)}, bf16[512,5120]{1,0:T(8,128)(2,1)S(1)}, u32[]{:S(2)}) %copy-start.1) | copy-done | bytes 5242904
  12.4 2.1 %collective-permute-start = (bf16[128,5120]{1,0:T(8,128)(2,1)S(1)}, bf16[128,5120]{1,0:T(8,128)(2,1)S(1)}, u32[]{:S(2)}, u32[]{:S(2)}) collective-permute-start(bf16[128,5120]{1,0:T(8,128)(2,1)S(1)} %get-tuple-element.6), channel_id=1, source_target_pairs={{0,1},{1,2},{2,3},{3,0},{4,5},{5,6},{6,7},{7,4},{8,9},{9,10},{10,1... | collective-permute-start | bytes 3932168 | tf_op jit(solution)/shard_map/ppermute | solution.py:67
  14.5 2.0 %collective-permute-start.1 = (bf16[128,5120]{1,0:T(8,128)(2,1)S(1)}, bf16[128,5120]{1,0:T(8,128)(2,1)}, u32[]{:S(2)}, u32[]{:S(2)}) collective-permute-start(bf16[128,5120]{1,0:T(8,128)(2,1)S(1)} %get-tuple-element.6), channel_id=1, source_target_pairs={{0,3},{1,0},{2,1},{3,2},{4,7},{5,4},{6,5},{7,6},{8,11},{9,8},{10,9... | collective-permute-start | bytes 3932168 | tf_op jit(solution)/shard_map/ppermute | solution.py:72
  16.5 28.5 %collective-permute-done = bf16[128,5120]{1,0:T(8,128)(2,1)S(1)} collective-permute-done((bf16[128,5120]{1,0:T(8,128)(2,1)S(1)}, bf16[128,5120]{1,0:T(8,128)(2,1)S(1)}, u32[]{:S(2)}, u32[]{:S(2)}) %collective-permute-start) | collective-permute-done | bytes 1310752 | tf_op jit(solution)/shard_map/ppermute | solution.py:67
  45.0 0.0 collective-permute-start.2
  45.0 0.0 copy-done.4
  45.0 0.1 reshape.73
  45.1 1.2 constant_dynamic-update-slice_fusion.2
  46.3 26.5 %collective-permute-done.1 = bf16[128,5120]{1,0:T(8,128)(2,1)} collective-permute-done((bf16[128,5120]{1,0:T(8,128)(2,1)S(1)}, bf16[128,5120]{1,0:T(8,128)(2,1)}, u32[]{:S(2)}, u32[]{:S(2)}) %collective-permute-start.1) | collective-permute-done | bytes 1310752 | tf_op jit(solution)/shard_map/ppermute | solution.py:72
  72.8 2.4 %constant_dynamic-update-slice_fusion.1 = bf16[512,5120]{1,0:T(8,128)(2,1)} fusion(bf16[512,5120]{1,0:T(8,128)(2,1)} %constant_dynamic-update-slice_fusion.2, bf16[128,5120]{1,0:T(8,128)(2,1)} %collective-permute-done.1, s32[]{:T(128)S(6)} %select_n.46), kind=kLoop, calls=%fused_computation.34 | loop fusion | bytes 2621444 | tf_op jit(solution)/shard_map/dynamic_update_slice | solution.py:73
  75.2 24.4 %collective-permute-done.2 = bf16[128,5120]{1,0:T(8,128)(2,1)} collective-permute-done((bf16[128,5120]{1,0:T(8,128)(2,1)S(1)}, bf16[128,5120]{1,0:T(8,128)(2,1)}, u32[]{:S(2)}, u32[]{:S(2)}) %collective-permute-start.2) | collective-permute-done | bytes 1310752 | tf_op jit(solution)/shard_map/ppermute | solution.py:67
  99.6 2.5 %constant_dynamic-update-slice_fusion = bf16[512,5120]{1,0:T(8,128)(2,1)} fusion(bf16[512,5120]{1,0:T(8,128)(2,1)} %constant_dynamic-update-slice_fusion.1, bf16[128,5120]{1,0:T(8,128)(2,1)} %collective-permute-done.2, s32[]{:T(128)S(6)} %select_n.48), kind=kLoop, calls=%fused_computation.33 | loop fusion | bytes 2621444 | tf_op jit(solution)/shard_map/dynamic_update_slice | solution.py:68
  102.1 0.0 copy-start.5
  102.1 0.0 all-gather.2.cloned.1.call-done
  102.1 9.0 %fusion.16 = bf16[3,512,256]{2,1,0:T(8,128)(2,1)S(1)} fusion(bf16[3,5120,256]{2,1,0:T(8,128)(2,1)} %all-gather.2.cloned.1.call-done, bf16[512,5120]{1,0:T(8,128)(2,1)} %constant_dynamic-update-slice_fusion), kind=kOutput, calls=%fused_computation.21 | convolution fusion | flops 4026925056 | bytes 13893632 | tf_op jit(solution)/shard_map/td,ide->ite/dot_general | solution.py:76
  111.2 5.9 %collective-permute-start.3 = (bf16[2,256,256]{2,1,0:T(8,128)(2,1)S(1)}, bf16[2,256,256]{2,1,0:T(8,128)(2,1)S(1)}, u32[]{:S(2)}, u32[]{:S(2)}) collective-permute-start(bf16[2,256,256]{2,1,0:T(8,128)(2,1)S(1)} %get-tuple-element.9), channel_id=1, source_target_pairs={{0,4},{4,8},{8,12},{1,5},{5,9},{9,13},{2,6},{6,10},{10,14},{3,7},{... | collective-permute-start | bytes 786440 | tf_op jit(solution)/shard_map/ppermute | solution.py:19
  117.1 1.9 %collective-permute-start.4 = (bf16[2,256,256]{2,1,0:T(8,128)(2,1)S(1)}, bf16[2,256,256]{2,1,0:T(8,128)(2,1)S(1)}, u32[]{:S(2)}, u32[]{:S(2)}) collective-permute-start(bf16[2,256,256]{2,1,0:T(8,128)(2,1)S(1)} %get-tuple-element.10), channel_id=1, source_target_pairs={{4,0},{8,4},{12,8},{5,1},{9,5},{13,9},{6,2},{10,6},{14,10},{7,3},{... | collective-permute-start | bytes 786440 | tf_op jit(solution)/shard_map/ppermute | solution.py:20
  119.1 0.0 copy-done.5
  119.1 0.1 iota_compare_fusion
  119.2 0.1 reshape_squeeze.10
  119.3 1.1 collective-permute-done.3
  120.4 4.4 %collective-permute-done.4 = bf16[2,256,256]{2,1,0:T(8,128)(2,1)S(1)} collective-permute-done((bf16[2,256,256]{2,1,0:T(8,128)(2,1)S(1)}, bf16[2,256,256]{2,1,0:T(8,128)(2,1)S(1)}, u32[]{:S(2)}, u32[]{:S(2)}) %collective-permute-start.4) | collective-permute-done | bytes 262176 | tf_op jit(solution)/shard_map/ppermute | solution.py:20
  124.8 0.1 pad_maximum_fusion
  124.9 0.1 fusion.33
  125.0 0.1 reshape_squeeze.11
  125.1 0.1 copy.15
  125.2 0.8 gather_fusion.1
  126.0 0.1 copy.17
  126.1 0.5 fusion.28
  126.6 0.4 fusion.8
  127.1 0.6 fusion.9
  127.7 0.9 reshape_squeeze.9
  128.6 1.1 copy.14
  129.7 1.9 %gather_fusion = bf16[20,128,2,128]{3,1,2,0:T(8,128)(2,1)} fusion(bf16[8,128,2,128]{3,1,2,0:T(8,128)(2,1)S(1)} %copy.14, s32[1024]{0:T(1024)S(1)} %pad_clamp_fusion), kind=kCustom, calls=%fused_computation | custom fusion | bytes 2621520 | tf_op jit(solution)/shard_map/gather | solution.py:32
  131.6 2.4 %fusion.25 = bf16[4,128,2,128]{1,3,2,0:T(8,128)(2,1)S(1)} fusion(f32[4,2,128,5,128]{2,4,3,1,0:T(8,128)S(1)} %bitcast.38, f32[4,2,128]{2,1,0:T(2,128)S(1)} %fusion.9, f32[4,2,128]{2,1,0:T(2,128)S(1)} %fusion.8, pred[4,5]{1,0:T(4,128)(4,1)S(1)} %iota_compare_fusion, bf16[4,5,128,2,128]{4,2,3,1,0:T(8,128)(2,1)} %bitcast.41), kind=kOutput, calls=%fused_computation.24 | convolution fusion | flops 171180032 | bytes 4202516 | tf_op jit(solution)/shard_map/phtks,pkshd->pthd/dot_general | solution.py:43
  134.0 0.2 copy.20
  134.2 0.7 copy.37
  (8 shorter events, 0.1 us)
Async XLA Ops:
  6.5 1.3 copy-start
  6.5 2.1 %copy-start.3 = (f32[5120]{0:T(1024)S(1)}, f32[5120]{0:T(1024)}, u32[]{:S(2)}) copy-start(f32[5120]{0:T(1024)} %param.8) | copy-start | bytes 61444
  6.5 95.6 %all-gather.2.cloned.1.call-start = ((), (), s32[]{:S(2)}) async-start(), calls=%async_computation | async-start | bytes 9830400 | tf_op jit(solution)/shard_map/all_gather | solution.py:79
  8.7 0.7 copy-start.2
  9.4 35.6 %copy-start.4 = (s32[1,4,5]{2,1,0:T(4,128)S(1)}, s32[1,4,5]{2,1,0:T(4,128)}, u32[]{:S(2)}) copy-start(s32[1,4,5]{2,1,0:T(4,128)} %param.10) | copy-start | bytes 244
  10.0 2.3 %copy-start.1 = (bf16[512,5120]{1,0:T(8,128)(2,1)}, bf16[512,5120]{1,0:T(8,128)(2,1)S(1)}, u32[]{:S(2)}) copy-start(bf16[512,5120]{1,0:T(8,128)(2,1)S(1)} %get-tuple-element.5) | copy-start | bytes 15728644
  12.4 32.7 %collective-permute-start = (bf16[128,5120]{1,0:T(8,128)(2,1)S(1)}, bf16[128,5120]{1,0:T(8,128)(2,1)S(1)}, u32[]{:S(2)}, u32[]{:S(2)}) collective-permute-start(bf16[128,5120]{1,0:T(8,128)(2,1)S(1)} %get-tuple-element.6), channel_id=1, source_target_pairs={{0,1},{1,2},{2,3},{3,0},{4,5},{5,6},{6,7},{7,4},{8,9},{9,10},{10,1... | collective-permute-start | bytes 3932168 | tf_op jit(solution)/shard_map/ppermute | solution.py:67
  14.5 58.3 %collective-permute-start.1 = (bf16[128,5120]{1,0:T(8,128)(2,1)S(1)}, bf16[128,5120]{1,0:T(8,128)(2,1)}, u32[]{:S(2)}, u32[]{:S(2)}) collective-permute-start(bf16[128,5120]{1,0:T(8,128)(2,1)S(1)} %get-tuple-element.6), channel_id=1, source_target_pairs={{0,3},{1,0},{2,1},{3,2},{4,7},{5,4},{6,5},{7,6},{8,11},{9,8},{10,9... | collective-permute-start | bytes 3932168 | tf_op jit(solution)/shard_map/ppermute | solution.py:72
  45.0 54.6 %collective-permute-start.2 = (bf16[128,5120]{1,0:T(8,128)(2,1)S(1)}, bf16[128,5120]{1,0:T(8,128)(2,1)}, u32[]{:S(2)}, u32[]{:S(2)}) collective-permute-start(bf16[128,5120]{1,0:T(8,128)(2,1)S(1)} %collective-permute-done), channel_id=1, source_target_pairs={{0,1},{1,2},{2,3},{3,0},{4,5},{5,6},{6,7},{7,4},{8,9},{9,10},{10,1... | collective-permute-start | bytes 3932168 | tf_op jit(solution)/shard_map/ppermute | solution.py:67
  102.1 17.0 %copy-start.5 = (s32[1,4]{1,0:T(1,128)S(1)}, s32[1,4]{1,0:T(1,128)}, u32[]{:S(2)}) copy-start(s32[1,4]{1,0:T(1,128)} %param.11) | copy-start | bytes 52
  111.2 9.2 %collective-permute-start.3 = (bf16[2,256,256]{2,1,0:T(8,128)(2,1)S(1)}, bf16[2,256,256]{2,1,0:T(8,128)(2,1)S(1)}, u32[]{:S(2)}, u32[]{:S(2)}) collective-permute-start(bf16[2,256,256]{2,1,0:T(8,128)(2,1)S(1)} %get-tuple-element.9), channel_id=1, source_target_pairs={{0,4},{4,8},{8,12},{1,5},{5,9},{9,13},{2,6},{6,10},{10,14},{3,7},{... | collective-permute-start | bytes 786440 | tf_op jit(solution)/shard_map/ppermute | solution.py:19
  117.1 7.7 %collective-permute-start.4 = (bf16[2,256,256]{2,1,0:T(8,128)(2,1)S(1)}, bf16[2,256,256]{2,1,0:T(8,128)(2,1)S(1)}, u32[]{:S(2)}, u32[]{:S(2)}) collective-permute-start(bf16[2,256,256]{2,1,0:T(8,128)(2,1)S(1)} %get-tuple-element.10), channel_id=1, source_target_pairs={{4,0},{8,4},{12,8},{5,1},{9,5},{13,9},{6,2},{10,6},{14,10},{7,3},{... | collective-permute-start | bytes 786440 | tf_op jit(solution)/shard_map/ppermute | solution.py:20
Sparse Core Ops, SparseCore 0:
  8.9 57.7 all-gather.1
